TPU v7x, 32 devices: a whole 2x2x4 slice. The times are simulated.
32 devices in a mesh: row: 16 (over z, y, x), col: 2 (over core).
Axes of the slice: x: 2, y: 2, z: 4, core: 2. Of those that a mesh axis runs over, the one named last changes fastest.
Arguments:
- tokens: bfloat16 [8192, 6144], P('row', 'col'), may hold values from -6 to 6
- w_blocks: bfloat16 [96, 81920], P('col', 'row'), may hold values from -0.25 to 0.25
- hidden_bias: bfloat16 [12288], P('col'), may hold values from -3 to 3
- pattern: int32 [96, 5], replicated, may hold values from 0 to 47, as said below
- grad_act: bfloat16 [8192, 12288], P('row', 'col'), may hold values from -6 to 6
Outputs:
- activation: bfloat16 [8192, 12288], P('row', 'col')
- weight_grad: float32 [96, 81920], P('col', 'row')
- bias_grad: float32 [12288], P('col')
Inputs may be any that keep to these rules, and one draw needn't show every extreme that they name: `pattern`: panel p holds input blocks p * 24 to (p + 1) * 24 - 1, and hidden block h lies in group g = h // 48. Slot 0 of h names a block in panel g; slot k for 1 <= k <= 3 names a block in panel (g + 2^(k-1)) mod 2; slot 4 names one of the blocks 0 to 1. Names may repeat within a hidden block.
All inputs are finite; a program needn't handle non-finite values.
Results may differ from a plain program's by a relative error of at most 0.003.
Values may be sent and summed in bfloat16 or wider, within the bound.
A program may use at most 192 MiB of HBM per device.

v0:
```python
import functools
import math

import jax
import jax.numpy as jnp
from jax import lax
from jax.experimental import pallas as pl
from jax.experimental.pallas import tpu as pltpu
from jax.sharding import PartitionSpec as P

BLK = 128
LEVELS = 3
GLOB = 2
KSLOT = 5
MESH = pl.DeviceIdType.MESH
VMEM_LIMIT = 60 * 1024 * 1024


def from_behind(block, axis, distance):
    devices = range(lax.axis_size(axis))
    route = [((i - distance) % len(devices), i) for i in devices]
    return lax.ppermute(block, axis, route)


def broadcast(value, axis, source):
    kept = jnp.where(lax.axis_index(axis) == source, value, 0).astype(value.dtype)
    return lax.psum(kept, axis)


def plain_body(tokens, w_blocks, hidden_bias, pattern, grad_act):
    tok_rows = tokens.shape[0]
    local_blocks = w_blocks.shape[0]
    col_count = lax.axis_size("col")
    col_index = lax.axis_index("col")
    panel_blocks = tokens.shape[1] // BLK
    inv_scale = 1.0 / math.sqrt(tok_rows * lax.axis_size("row"))
    gathered_weights = lax.all_gather(w_blocks, "row", axis=1, tiled=True)
    weights = gathered_weights.reshape(local_blocks, KSLOT, BLK, BLK)
    my_pattern = lax.dynamic_slice_in_dim(pattern, col_index * local_blocks, local_blocks, 0)
    own_panel = tokens.reshape(tok_rows, panel_blocks, BLK)
    pieces = [jnp.take(own_panel, my_pattern[:, 0] - col_index * panel_blocks, axis=1)]
    for level_index in range(LEVELS):
        offset = 2**level_index % col_count
        if offset == 0:
            source = own_panel
        else:
            moved = from_behind(tokens, "col", -offset)
            source = moved.reshape(tok_rows, panel_blocks, BLK)
        home_panel = (col_index + offset) % col_count
        pieces.append(
            jnp.take(source, my_pattern[:, level_index + 1] - home_panel * panel_blocks, axis=1)
        )
    shared = broadcast(tokens[:, : GLOB * BLK], "col", 0).reshape(tok_rows, GLOB, BLK)
    pieces.append(jnp.take(shared, my_pattern[:, LEVELS + 1], axis=1))
    picked = jnp.stack(pieces, axis=2)
    pre_act = jnp.einsum("thkc,hkcd->thd", picked, weights, preferred_element_type=jnp.float32)
    pre_act = pre_act + hidden_bias.astype(jnp.float32).reshape(local_blocks, BLK)
    act_value, pull_back = jax.vjp(jax.nn.gelu, pre_act)
    activation = act_value.reshape(tok_rows, local_blocks * BLK).astype(jnp.bfloat16)
    grad_pre = pull_back(grad_act.astype(jnp.float32).reshape(tok_rows, local_blocks, BLK))[0]
    grad_rounded = grad_pre.astype(jnp.bfloat16)
    weight_terms = (
        jnp.einsum("thkc,thd->hkcd", picked, grad_rounded, preferred_element_type=jnp.float32)
        * inv_scale
    )
    weight_terms = weight_terms.reshape(local_blocks, KSLOT * BLK * BLK)
    weight_grad = lax.psum_scatter(weight_terms, "row", scatter_dimension=1, tiled=True)
    bias_terms = jnp.sum(grad_pre, axis=0).reshape(local_blocks * BLK) * inv_scale
    bias_grad = lax.psum(bias_terms, "row")
    return (activation, weight_grad, bias_grad)


def place(quads):
    row = lax.axis_index("row")
    return row, row // 4, (row // 2) % 2, row % 2, lax.axis_index("col")


def greet(row, quad, bit_y, bit_x, col, quads, extra=()):
    barrier = pltpu.get_barrier_semaphore()
    peers = [(quad * 4 + bit_y * 2 + 1 - bit_x, col), (quad * 4 + (1 - bit_y) * 2 + bit_x, col)]
    peers += [((quad + d) % quads * 4 + bit_y * 2 + bit_x, col) for d in range(1, quads)]
    peers += list(extra)
    for peer in peers:
        pl.semaphore_signal(barrier, inc=1, device_id=peer, device_id_type=MESH)
    pl.semaphore_wait(barrier, len(peers))


def gather_kernel(quads, w_ref, tok_ref, all_ref, peer_ref,
                  own_sem, tok_s, tok_r, z_s, z_r, y_s, y_r, x_s, x_r):
    row, quad, bit_y, bit_x, col = place(quads)
    half = w_ref.shape[0] // 2
    x_peer = (quad * 4 + bit_y * 2 + 1 - bit_x, col)
    y_peer = (quad * 4 + (1 - bit_y) * 2 + bit_x, col)
    greet(row, quad, bit_y, bit_x, col, quads, [(row, 1 - col)])

    def send(src, dst, s, r, peer):
        copy = pltpu.make_async_remote_copy(
            src_ref=src, dst_ref=dst, send_sem=s, recv_sem=r, device_id=peer, device_id_type=MESH
        )
        copy.start()
        return copy

    copies = []
    own = pltpu.make_async_copy(w_ref, all_ref.at[row], own_sem)
    own.start()
    z_copies = {}

    def send_quad(d):
        target = ((quad + d) % quads * 4 + bit_y * 2 + bit_x, col)
        z_copies[d] = send(w_ref, all_ref.at[row], z_s.at[d - 1], z_r.at[d - 1], target)

    order = sorted(range(quads), key=lambda d: min(d, quads - d))
    send_quad(order[1])
    cut = [pl.ds(0, half), pl.ds(half, half)]
    first_y, first_x = {}, {}

    def relay(d):
        from_quad = (quad - d + quads) % quads * 4
        y_row = from_quad + (1 - bit_y) * 2 + bit_x
        x_row = from_quad + bit_y * 2 + 1 - bit_x
        first_y[d].wait_recv()
        piece = all_ref.at[y_row, cut[0]]
        copies.append(send(piece, piece, x_s.at[2 * quads + d], x_r.at[2 * quads + d], x_peer))
        first_x[d].wait_recv()
        piece = all_ref.at[x_row, cut[1]]
        copies.append(send(piece, piece, y_s.at[2 * quads + d], y_r.at[2 * quads + d], y_peer))

    for i, d in enumerate(order):
        src_row = (quad - d + quads) % quads * 4 + bit_y * 2 + bit_x
        if i > 0:
            z_copies[d].wait_recv()
            if i + 1 < quads:
                send_quad(order[i + 1])
        src = [w_ref.at[c] if d == 0 else all_ref.at[src_row, c] for c in cut]
        dst = [all_ref.at[src_row, c] for c in cut]
        first_y[d] = send(src[0], dst[0], y_s.at[d], y_r.at[d], y_peer)
        first_x[d] = send(src[1], dst[1], x_s.at[d], x_r.at[d], x_peer)
        copies.append(send(src[0], dst[0], x_s.at[quads + d], x_r.at[quads + d], x_peer))
        copies.append(send(src[1], dst[1], y_s.at[quads + d], y_r.at[quads + d], y_peer))
        if i == 0:
            tok_copy = send(tok_ref, peer_ref, tok_s, tok_r, (row, 1 - col))
        else:
            relay(order[i - 1])
    relay(order[-1])
    for copy in copies:
        copy.wait()
    for copy in [*z_copies.values(), *first_y.values(), *first_x.values()]:
        copy.wait_send()
    tok_copy.wait()
    own.wait()


def gather(w_flat, tokens, quads):
    any_spec = pl.BlockSpec(memory_space=pl.ANY)
    dma = pltpu.SemaphoreType.DMA
    return pl.pallas_call(
        functools.partial(gather_kernel, quads),
        out_shape=(
            jax.ShapeDtypeStruct((quads * 4,) + w_flat.shape, w_flat.dtype),
            jax.ShapeDtypeStruct(tokens.shape, tokens.dtype),
        ),
        in_specs=[pl.BlockSpec(memory_space=pltpu.VMEM), any_spec],
        out_specs=(any_spec, any_spec),
        scratch_shapes=[dma, dma, dma, dma((quads - 1,)), dma((quads - 1,)),
                        dma((3 * quads,)), dma((3 * quads,)), dma((3 * quads,)), dma((3 * quads,))],
        compiler_params=pltpu.CompilerParams(collective_id=0, has_side_effects=True,
                                             vmem_limit_bytes=VMEM_LIMIT),
    )(w_flat, tokens)


def fused_kernel(quads, chunks, blk_rows, strip, scale,
                 pat_ref, own_ref, peer_ref, w_ref, bias_ref, grad_ref,
                 act_ref, out_ref, bout_ref,
                 table, p_ref, b_ref, first, second, second_out, third, third_out,
                 bx, by, by_out, bz, bz_out,
                 f_s, f_r, s_s, s_r, t_s, t_r, b_s, b_r):
    step = pl.program_id(0)
    steps = pl.num_programs(0)
    rows = quads * 4
    row, quad, bit_y, bit_x, col = place(quads)
    n = first.shape[3]
    half = p_ref.shape[1] // 2
    per = p_ref.shape[1] // chunks // (2 * blk_rows)
    peers = [(quad * 4 + bit_y * 2 + 1 - bit_x, col), (quad * 4 + (1 - bit_y) * 2 + bit_x, col)]

    @pl.when(step == 0)
    def _():
        greet(row, quad, bit_y, bit_x, col, quads)

        panel = own_ref.shape[1] // BLK
        for i in range(panel):
            table[col * panel + i] = own_ref[:, i * BLK:(i + 1) * BLK]
            table[(1 - col) * panel + i] = peer_ref[:, i * BLK:(i + 1) * BLK]

    pair = pair_of(step, per, chunks)
    weights = [w_ref[r].astype(jnp.float32) for r in range(rows)]
    results = []
    for j in range(2):
        piece = pl.ds(j * BLK, BLK)
        w = jnp.concatenate([v[j * blk_rows:(j + 1) * blk_rows] for v in weights], axis=0)
        w = w.astype(jnp.bfloat16)
        base = (2 * pair + j) * KSLOT
        picks = [table[pat_ref[base + k]] for k in range(KSLOT)]
        sel = jnp.concatenate(picks, axis=1)
        v = jnp.dot(sel, w, preferred_element_type=jnp.float32)
        v = v + bias_ref[:, piece].astype(jnp.float32)
        c = math.sqrt(2.0 / math.pi)
        sq = v * v
        t = jnp.tanh(v * (c + (c * 0.044715) * sq))
        lift = 0.5 + 0.5 * t
        act_ref[:, piece] = (v * lift).astype(jnp.bfloat16)
        slope = lift + (0.5 * v) * (1.0 - t * t) * (c + (3.0 * 0.044715 * c) * sq)
        grad = grad_ref[:, piece].astype(jnp.float32) * slope
        b_ref[pl.ds(2 * pair + j, 1), :] = jnp.sum(grad, axis=0, keepdims=True) * scale
        out = lax.dot_general(sel, grad.astype(jnp.bfloat16), (((0,), (0,)), ((), ())),
                              preferred_element_type=jnp.float32)
        results.append(out * scale)
    at = pl.multiple_of(pair * (2 * blk_rows), 2 * blk_rows)
    for r in range(rows):
        cut = slice(r * blk_rows, (r + 1) * blk_rows)
        p_ref[r, pl.ds(at, 2 * blk_rows), :] = jnp.concatenate(
            [o[cut] for o in results], axis=0).astype(p_ref.dtype)

    def link(src, dst, s, r, peer):
        return pltpu.make_async_remote_copy(
            src_ref=src, dst_ref=dst, send_sem=s, recv_sem=r, device_id=peer, device_id_type=MESH
        )

    def piece_row(d, colour, near, far):
        flip_x, flip_y = (near, far) if colour == 0 else (far, near)
        x = (1 - bit_x) if flip_x else bit_x
        y = (1 - bit_y) if flip_y else bit_y
        return (quad + d) % quads * 4 + y * 2 + x

    order = list(range(1, quads)) + [0]
    start = lambda c: (c % 2) * half + (c // 2) * n

    def first_copy(c, far, d):
        return link(p_ref.at[piece_row(d, c % 2, 1, far), pl.ds(start(c), n)],
                    first.at[c, far, d], f_s.at[c, far, d], f_r.at[c, far, d], peers[c % 2])

    def second_copy(c, d):
        return link(second_out.at[c, d], second.at[c, d], s_s.at[c, d], s_r.at[c, d],
                    peers[1 - c % 2])

    def third_copy(c, d):
        target = ((quad + d) % quads * 4 + bit_y * 2 + bit_x, col)
        return link(third_out.at[c, d - 1], third.at[c, d - 1],
                    t_s.at[c, d - 1], t_r.at[c, d - 1], target)

    def do_first(c):
        for far in (1, 0):
            for d in order:
                first_copy(c, far, d).start()

    def do_second(c):
        for d in order:
            first_copy(c, 1, d).wait_recv()
            mine = piece_row(d, c % 2, 0, 1)

            @pl.loop(0, n // strip)
            def _(i, d=d, mine=mine):
                s = pl.multiple_of(i * strip, strip)
                here = p_ref[mine, pl.ds(start(c) + s, strip), :].astype(jnp.float32)
                come = first[c, 1, d, pl.ds(s, strip), :].astype(jnp.float32)
                second_out[c, d, pl.ds(s, strip), :] = (here + come).astype(jnp.bfloat16)

            second_copy(c, d).start()

    def do_third(c):
        for d in order:
            first_copy(c, 0, d).wait_recv()
            second_copy(c, d).wait_recv()
            mine = piece_row(d, c % 2, 0, 0)

            @pl.loop(0, n // strip)
            def _(i, d=d, mine=mine):
                s = pl.multiple_of(i * strip, strip)
                total = p_ref[mine, pl.ds(start(c) + s, strip), :].astype(jnp.float32)
                total += first[c, 0, d, pl.ds(s, strip), :].astype(jnp.float32)
                total += second[c, d, pl.ds(s, strip), :].astype(jnp.float32)
                if d == 0:
                    out_ref[pl.ds(start(c) + s, strip), :] = total
                else:
                    third_out[c, d - 1, pl.ds(s, strip), :] = total.astype(jnp.bfloat16)

            if d > 0:
                third_copy(c, d).start()

    for c in range(chunks):
        @pl.when(step == (c + 1) * per - 1)
        def _(c=c):
            do_first(c)
            if c >= 2:
                do_second(c - 2)
            if c >= 4:
                do_third(c - 4)

    @pl.when(step == steps - 1)
    def _():
        to_x = link(b_ref, bx, b_s.at[0], b_r.at[0], peers[0])
        to_x.start()
        do_second(chunks - 2)
        do_third(chunks - 4)
        to_x.wait()
        by_out[...] = b_ref[...] + bx[...]
        to_y = link(by_out, by, b_s.at[1], b_r.at[1], peers[1])
        to_y.start()
        do_second(chunks - 1)
        do_third(chunks - 3)
        to_y.wait()
        bz_out[...] = by_out[...] + by[...]
        to_z = []
        for d in range(1, quads):
            target = ((quad + d) % quads * 4 + bit_y * 2 + bit_x, col)
            to_z.append(link(bz_out, bz.at[d - 1], b_s.at[d + 1], b_r.at[d + 1], target))
            to_z[-1].start()
        do_third(chunks - 2)
        do_third(chunks - 1)
        for copy in to_z:
            copy.wait()
        total = bz_out[...]
        for d in range(quads - 1):
            total += bz[d]
        bout_ref[...] = total
        for c in range(chunks):
            for d in range(1, quads):
                third_copy(c, d).wait()

            @pl.loop(0, n // strip)
            def _(i, c=c):
                s = pl.multiple_of(i * strip, strip)
                total = out_ref[pl.ds(start(c) + s, strip), :]
                for d in range(quads - 1):
                    total += third[c, d, pl.ds(s, strip), :].astype(jnp.float32)
                out_ref[pl.ds(start(c) + s, strip), :] = total
        for c in range(chunks):
            for d in order:
                first_copy(c, 0, d).wait_send()
                first_copy(c, 1, d).wait_send()
                second_copy(c, d).wait_send()


def pair_of(step, per, chunks):
    chunk = step // per
    return (chunk % 2) * (per * chunks // 2) + (chunk // 2) * per + step % per


def fused(pat, own, peer, weights, bias, grad_act, quads, scale):
    tok, hidden = grad_act.shape
    blocks = hidden // BLK
    steps = blocks // 2
    total_rows = weights.shape[1]
    chunks = 8 if steps % 8 == 0 and total_rows % 128 == 0 else 4
    per = steps // chunks
    blk_rows = total_rows // blocks
    n = total_rows // chunks
    strip = next(c for c in (240, 160, 128, 96, 80, 64, 48, 32, 16) if n % c == 0)
    rows = quads * 4
    whole = lambda a: pl.BlockSpec(a.shape, lambda i, p: (0, 0))
    wide = lambda m: pl.BlockSpec((m, 2 * BLK), lambda i, p: (0, pair_of(i, per, chunks)))
    fixed = lambda *s: pl.BlockSpec(s, lambda i, p: (0, 0))
    cube = pl.BlockSpec((rows, 2 * blk_rows, BLK), lambda i, p: (0, pair_of(i, per, chunks), 0))
    dma = pltpu.SemaphoreType.DMA
    bf = lambda *s: pltpu.VMEM(s, jnp.bfloat16)
    f32 = lambda *s: pltpu.VMEM(s, jnp.float32)
    b = (blocks, BLK)
    return pl.pallas_call(
        functools.partial(fused_kernel, quads, chunks, blk_rows, strip, scale),
        out_shape=(
            jax.ShapeDtypeStruct((tok, hidden), jnp.bfloat16),
            jax.ShapeDtypeStruct((total_rows, BLK), jnp.float32),
            jax.ShapeDtypeStruct(b, jnp.float32),
        ),
        grid_spec=pltpu.PrefetchScalarGridSpec(
            num_scalar_prefetch=1, grid=(steps,),
            in_specs=[whole(own), whole(peer), cube, wide(1), wide(tok)],
            out_specs=[wide(tok), fixed(total_rows, BLK), fixed(*b)],
            scratch_shapes=[
                bf(2 * own.shape[1] // BLK, tok, BLK), bf(rows, total_rows, BLK), f32(*b),
                bf(chunks, 2, quads, n, BLK), bf(chunks, quads, n, BLK), bf(chunks, quads, n, BLK),
                bf(chunks, quads - 1, n, BLK), bf(chunks, quads - 1, n, BLK),
                f32(*b), f32(*b), f32(*b), f32(quads - 1, *b), f32(*b),
                dma((chunks, 2, quads)), dma((chunks, 2, quads)), dma((chunks, quads)),
                dma((chunks, quads)), dma((chunks, quads - 1)), dma((chunks, quads - 1)),
                dma((quads + 1,)), dma((quads + 1,)),
            ],
        ),
        compiler_params=pltpu.CompilerParams(collective_id=1, has_side_effects=True,
                                             vmem_limit_bytes=VMEM_LIMIT),
    )(pat, own, peer, weights, bias, grad_act)


def kernel_body(tokens, w_blocks, hidden_bias, pattern, grad_act):
    tok_rows = tokens.shape[0]
    local_blocks, width = w_blocks.shape
    rows = lax.axis_size("row")
    quads = rows // 4
    col = lax.axis_index("col")
    scale = 1.0 / math.sqrt(tok_rows * rows)
    pat = lax.dynamic_slice_in_dim(pattern, col * local_blocks, local_blocks, 0).reshape(-1)
    flat = w_blocks.reshape(local_blocks * width // BLK, BLK)
    weights, peer = gather(flat, tokens, quads)
    activation, weight_grad, bias_grad = fused(
        pat, tokens, peer, weights, hidden_bias.reshape(1, -1), grad_act, quads, scale)
    return activation, weight_grad.reshape(local_blocks, width), bias_grad.reshape(-1)


def body(tokens, w_blocks, hidden_bias, pattern, grad_act):
    rows = lax.axis_size("row")
    piece = w_blocks.shape[1] // BLK
    fits = lax.axis_size("col") == 2 and rows % 4 == 0 and rows > 4
    fits = fits and piece % 8 == 0 and w_blocks.shape[0] % 8 == 0
    run = kernel_body if fits else plain_body
    return run(tokens, w_blocks, hidden_bias, pattern, grad_act)


def solution(mesh):
    return jax.shard_map(
        body,
        mesh=mesh,
        in_specs=(P("row", "col"), P("col", "row"), P("col"), P(), P("row", "col")),
        out_specs=(P("row", "col"), P("col", "row"), P("col")),
        check_vma=False,
    )
```

profile of v0, /device:TPU:0, one launch (start us, length us, event | category | flops | bytes accessed | tf_op | source)
XLA Modules:
  0.0 187.4 jit_solution(6344416009363778227)
XLA Ops:
  0.6 0.0 copy-start
  0.6 0.7 copy-done
  1.3 0.1 constant_dynamic-slice_fusion
  1.4 0.1 copy.8
  1.5 0.7 reshape.21.pat_ref
  2.2 1.3 reshape.23.bias_ref
  3.5 2.0 %reshape.22.w_ref = bf16[1920,128]{1,0:T(8,128)(2,1)} reshape(bf16[48,5120]{1,0:T(8,128)(2,1)} %param.6) | data formatting | bytes 983040 | tf_op jit(solution)/shard_map/reshape | solution.py:402
  5.5 73.5 %shard_map.76 = (bf16[16,1920,128]{2,1,0:T(8,128)(2,1)}, bf16[512,3072]{1,0:T(8,128)(2,1)}) custom-call(bf16[1920,128]{1,0:T(8,128)(2,1)} %reshape.22.w_ref, bf16[512,3072]{1,0:T(8,128)(2,1)} %own_ref.1), custom_call_target="tpu_custom_call" | custom-call | tf_op jit(solution)/shard_map/pallas_call | solution.py:156
  79.0 99.2 %shard_map.77 = (bf16[512,6144]{1,0:T(8,128)(2,1)}, f32[1920,128]{1,0:T(8,128)}, f32[48,128]{1,0:T(8,128)}) custom-call(s32[240]{0:T(256)} %reshape.21.pat_ref, bf16[512,3072]{1,0:T(8,128)(2,1)} %own_ref.1, bf16[512,3072]{1,0:T(8,128)(2,1)} %get-tuple-element.8.peer_ref, bf16[16,1920,128]{2,1,0:T(8,128)(2,1)} %get-tuple-element.9.w_ref, ...), custom_call_target="tpu_custom_call" | custom-call | tf_op jit(solution)/shard_map/pallas_call | solution.py:368
  178.2 2.3 %reshape.24 = f32[48,5120]{1,0:T(8,128)} reshape(f32[1920,128]{1,0:T(8,128)} %get-tuple-element.11) | data formatting | bytes 1966080 | tf_op jit(solution)/shard_map/reshape | solution.py:406
  180.5 0.0 copy-start.1
  180.5 6.2 %copy.11 = bf16[512,6144]{1,0:T(8,128)(2,1)} copy(bf16[512,6144]{1,0:T(8,128)(2,1)} %get-tuple-element.16) | data formatting | bytes 12582912
  186.8 0.0 copy-done.1
  186.8 0.6 copy.12
Async XLA Ops:
  0.6 0.7 copy-start
  180.5 6.2 %copy-start.1 = (f32[48,128]{1,0:T(8,128)S(1)}, f32[48,128]{1,0:T(8,128)}, u32[]{:S(2)}) copy-start(f32[48,128]{1,0:T(8,128)} %get-tuple-element.12) | copy-start | bytes 73732
where the time goes:
time: 188 us; the launch traced here: 187 us
  Pallas kernels  173 us (92%)
  local copies, waits for them, and re-layouts  14 us (7%)
    pallas_call x1, Pallas kernels, fused(): pl.pallas_call(functools.partial(fused_kernel, quads, chunks, blk_rows, s...  99.2 us
    pallas_call x1, Pallas kernels, gather(): pl.pallas_call(functools.partial(gather_kernel, quads), out_shape=(jax.Sh...  73.5 us
    unnamed x6, local copies, waits for them, and re-layouts  7.53 us

commit v1 on v0

v1 whole, which is shorter than its diff:
```python
import functools
import math

import jax
import jax.numpy as jnp
from jax import lax
from jax.experimental import pallas as pl
from jax.experimental.pallas import tpu as pltpu
from jax.sharding import PartitionSpec as P

BLK = 128
LEVELS = 3
GLOB = 2
KSLOT = 5
MESH = pl.DeviceIdType.MESH
VMEM_LIMIT = 60 * 1024 * 1024


def from_behind(block, axis, distance):
    devices = range(lax.axis_size(axis))
    route = [((i - distance) % len(devices), i) for i in devices]
    return lax.ppermute(block, axis, route)


def broadcast(value, axis, source):
    kept = jnp.where(lax.axis_index(axis) == source, value, 0).astype(value.dtype)
    return lax.psum(kept, axis)


def plain_body(tokens, w_blocks, hidden_bias, pattern, grad_act):
    tok_rows = tokens.shape[0]
    local_blocks = w_blocks.shape[0]
    col_count = lax.axis_size("col")
    col_index = lax.axis_index("col")
    panel_blocks = tokens.shape[1] // BLK
    inv_scale = 1.0 / math.sqrt(tok_rows * lax.axis_size("row"))
    gathered_weights = lax.all_gather(w_blocks, "row", axis=1, tiled=True)
    weights = gathered_weights.reshape(local_blocks, KSLOT, BLK, BLK)
    my_pattern = lax.dynamic_slice_in_dim(pattern, col_index * local_blocks, local_blocks, 0)
    own_panel = tokens.reshape(tok_rows, panel_blocks, BLK)
    pieces = [jnp.take(own_panel, my_pattern[:, 0] - col_index * panel_blocks, axis=1)]
    for level_index in range(LEVELS):
        offset = 2**level_index % col_count
        if offset == 0:
            source = own_panel
        else:
            moved = from_behind(tokens, "col", -offset)
            source = moved.reshape(tok_rows, panel_blocks, BLK)
        home_panel = (col_index + offset) % col_count
        pieces.append(
            jnp.take(source, my_pattern[:, level_index + 1] - home_panel * panel_blocks, axis=1)
        )
    shared = broadcast(tokens[:, : GLOB * BLK], "col", 0).reshape(tok_rows, GLOB, BLK)
    pieces.append(jnp.take(shared, my_pattern[:, LEVELS + 1], axis=1))
    picked = jnp.stack(pieces, axis=2)
    pre_act = jnp.einsum("thkc,hkcd->thd", picked, weights, preferred_element_type=jnp.float32)
    pre_act = pre_act + hidden_bias.astype(jnp.float32).reshape(local_blocks, BLK)
    act_value, pull_back = jax.vjp(jax.nn.gelu, pre_act)
    activation = act_value.reshape(tok_rows, local_blocks * BLK).astype(jnp.bfloat16)
    grad_pre = pull_back(grad_act.astype(jnp.float32).reshape(tok_rows, local_blocks, BLK))[0]
    grad_rounded = grad_pre.astype(jnp.bfloat16)
    weight_terms = (
        jnp.einsum("thkc,thd->hkcd", picked, grad_rounded, preferred_element_type=jnp.float32)
        * inv_scale
    )
    weight_terms = weight_terms.reshape(local_blocks, KSLOT * BLK * BLK)
    weight_grad = lax.psum_scatter(weight_terms, "row", scatter_dimension=1, tiled=True)
    bias_terms = jnp.sum(grad_pre, axis=0).reshape(local_blocks * BLK) * inv_scale
    bias_grad = lax.psum(bias_terms, "row")
    return (activation, weight_grad, bias_grad)


def fused_kernel(quads, chunks, blk_rows, scale, hop,
                 pat_ref, tok_ref, w_ref, bias_ref, grad_ref,
                 act_ref, out_ref, bout_ref,
                 table, wbuf, part, psend, arecv, zout, zrecv, bsend, brecv,
                 b_ref, bx, by, by_out, bz, bz_out,
                 tl_s, t_s, t_r, lw_s, gb_s, gb_r, gz_s, gz_r, ga_s, ga_r,
                 ra_s, ra_r, rz_s, rz_r, rb_s, rb_r, b_s, b_r):
    step = pl.program_id(0)
    n = wbuf.shape[2]
    pairs = chunks * n // (2 * blk_rows)
    span = 2 * pairs // chunks
    rows = quads * 4
    row = lax.axis_index("row")
    col = lax.axis_index("col")
    z, y, x = row // 4, (row // 2) % 2, row % 2
    x_row = z * 4 + y * 2 + 1 - x
    y_row = z * 4 + (1 - y) * 2 + x
    panel = tok_ref.shape[1] // BLK
    begin = first_block(quads, hop)
    last = begin + 2 * pairs

    def link(src, dst, s, r, target):
        return pltpu.make_async_remote_copy(
            src_ref=src, dst_ref=dst, send_sem=s, recv_sem=r,
            device_id=(target, col), device_id_type=MESH
        )

    def local_token(i):
        return pltpu.make_async_copy(
            tok_ref.at[:, pl.ds(i * BLK, BLK)], table.at[col * panel + i], tl_s)

    def far_token(i):
        return pltpu.make_async_remote_copy(
            src_ref=tok_ref.at[:, pl.ds(i * BLK, BLK)], dst_ref=table.at[col * panel + i],
            send_sem=t_s, recv_sem=t_r, device_id=(row, 1 - col), device_id_type=MESH)

    def sides(c):
        k = c % 2
        a = y + k * (x - y)
        b = x + k * (y - x)
        return a, b, y_row + k * (x_row - y_row), x_row + k * (y_row - x_row)

    def pair_at(side, plane):
        return pl.ds((side * quads + plane) * 2, 2)

    def spot(side, plane, b):
        return (side * quads + plane) * 2 + b

    def load_weight(c):
        a, b, _, _ = sides(c)
        return pltpu.make_async_copy(w_ref.at[c], wbuf.at[c, spot(a, z, b)], lw_s.at[c])

    def gather_near(c):
        a, b, _, b_row = sides(c)
        here = wbuf.at[c, spot(a, z, b)]
        return link(here, here, gb_s, gb_r.at[c], b_row)

    def gather_z(c, plane, up):
        a, _, _, _ = sides(c)
        here = wbuf.at[c, pair_at(a, plane)]
        return link(here, here, gz_s.at[c, up, plane], gz_r.at[c, plane], row + (8 * up - 4))

    def gather_far(c, plane):
        a, _, a_row, _ = sides(c)
        here = wbuf.at[c, pair_at(a, plane)]
        return link(here, here, ga_s, ga_r.at[c, plane], a_row)

    def scatter_far(c, plane):
        _, _, a_row, _ = sides(c)
        return link(psend.at[c, pl.ds(plane * 2, 2)], arecv.at[c, pl.ds(plane * 2, 2)],
                    ra_s, ra_r.at[c, plane], a_row)

    def scatter_z(c, plane, up, slot):
        return link(zout.at[c, pl.ds(plane * 2, 2)], zrecv.at[c, pl.ds(slot * 2, 2)],
                    rz_s.at[c, plane], rz_r.at[c, slot], row + (8 * up - 4))

    def scatter_near(c):
        _, _, _, b_row = sides(c)
        return link(bsend.at[c], brecv.at[c], rb_s, rb_r.at[c], b_row)

    def gather_hop(c, i):
        if i == 0:
            gather_near(c).wait_recv()
            pl.when(z < quads - 1)(lambda: gather_z(c, z, 1).start())
            pl.when(z > 0)(lambda: gather_z(c, z, 0).start())
            gather_far(c, z).start()
            return

        @pl.when(z - i >= 0)
        def _():
            gather_z(c, z - i, 1).wait_recv()
            pl.when(z < quads - 1)(lambda: gather_z(c, z - i, 1).start())
            gather_far(c, z - i).start()

        @pl.when(z + i < quads)
        def _():
            gather_z(c, z + i, 0).wait_recv()
            pl.when(z > 0)(lambda: gather_z(c, z + i, 0).start())
            gather_far(c, z + i).start()

    def scatter_first(c):
        a, _, _, _ = sides(c)

        def go(plane):
            psend[c, pl.ds(plane * 2, 2)] = part[c, pair_at(1 - a, plane)].astype(jnp.bfloat16)
            scatter_far(c, plane).start()

        for i in reversed(range(1, quads)):
            pl.when(z + i < quads)(lambda i=i: go(z + i))
            pl.when(z - i >= 0)(lambda i=i: go(z - i))
        go(z)

    def scatter_hop(c, i):
        a, b, _, _ = sides(c)

        def pass_on(plane, up, chained):
            scatter_far(c, plane).wait_recv()
            mine = part[c, pair_at(a, plane)] + arecv[c, pl.ds(plane * 2, 2)].astype(jnp.float32)

            @pl.when(chained)
            def _():
                scatter_z(c, plane, up, plane).wait_recv()
                zout[c, pl.ds(plane * 2, 2)] = (
                    mine + zrecv[c, pl.ds(plane * 2, 2)].astype(jnp.float32)).astype(jnp.bfloat16)

            @pl.when(jnp.logical_not(chained))
            def _():
                zout[c, pl.ds(plane * 2, 2)] = mine.astype(jnp.bfloat16)

            slot = quads if up == 0 and i == 1 else plane
            scatter_z(c, plane, up, slot).start()

        if i > 0:
            pl.when(z + i < quads)(lambda: pass_on(z + i, 1, z > 0))
            pl.when(z - i >= 0)(lambda: pass_on(z - i, 0, z < quads - 1))
            return
        scatter_far(c, z).wait_recv()
        own = pair_at(a, z)
        part[c, own] = part[c, own] + arecv[c, pl.ds(z * 2, 2)].astype(jnp.float32)

        @pl.when(z > 0)
        def _():
            scatter_z(c, z, 1, z).wait_recv()
            part[c, own] = part[c, own] + zrecv[c, pl.ds(z * 2, 2)].astype(jnp.float32)

        @pl.when(z < quads - 1)
        def _():
            scatter_z(c, z, 0, quads).wait_recv()
            part[c, own] = part[c, own] + zrecv[c, pl.ds(quads * 2, 2)].astype(jnp.float32)

        bsend[c] = part[c, spot(a, z, 1 - b)].astype(jnp.bfloat16)
        scatter_near(c).start()

    def scatter_last(c):
        a, b, _, _ = sides(c)
        scatter_near(c).wait_recv()
        total = part[c, spot(a, z, b)] + brecv[c].astype(jnp.float32)
        out_ref[pl.ds(pl.multiple_of(c * n, n), n), :] = total * scale

    def gathered(c):
        for plane in range(quads):
            gather_far(c, plane).wait_recv()

    def compute(block, j):
        c = block // span
        base = (col * 2 * pairs + block) * KSLOT
        skip = j * blk_rows // 16 * 16
        tall = -(-(j * blk_rows - skip + blk_rows) // 16) * 16
        cut = slice(j * blk_rows - skip, j * blk_rows - skip + blk_rows)
        inner = (block % span) // 2 * (2 * blk_rows)
        at = pl.multiple_of(inner + skip, 16)
        k = c % 2
        spots = []
        for r in range(rows):
            q, v, u = r // 4, (r // 2) % 2, r % 2
            spots.append(spot(v + k * (u - v), q, u + k * (v - u)))
        w = [wbuf[c, s, pl.ds(at, tall), :].astype(jnp.float32)[cut] for s in spots]
        w = jnp.concatenate(w, axis=0).astype(jnp.bfloat16)
        piece = pl.ds(j * BLK, BLK)
        picks = [table[pat_ref[base + s]] for s in range(KSLOT)]
        sel = jnp.concatenate(picks, axis=1)
        v = jnp.dot(sel, w, preferred_element_type=jnp.float32)
        v = v + bias_ref[:, piece].astype(jnp.float32)
        e = math.sqrt(2.0 / math.pi)
        sq = v * v
        t = jnp.tanh(v * (e + (e * 0.044715) * sq))
        lift = 0.5 + 0.5 * t
        act_ref[:, piece] = (v * lift).astype(jnp.bfloat16)
        slope = lift + (0.5 * v) * (1.0 - t * t) * (e + (3.0 * 0.044715 * e) * sq)
        grad = grad_ref[:, piece].astype(jnp.float32) * slope
        b_ref[pl.ds(block, 1), :] = jnp.sum(grad, axis=0, keepdims=True) * scale
        out = lax.dot_general(sel, grad.astype(jnp.bfloat16), (((0,), (0,)), ((), ())),
                              preferred_element_type=jnp.float32)
        put = pl.ds(pl.multiple_of(inner + j * blk_rows, 8), blk_rows)
        for r in range(rows):
            part[c, spots[r], put, :] = out[r * blk_rows:(r + 1) * blk_rows]

    def swap(src, dst, i, target):
        return link(src, dst, b_s.at[i], b_r.at[i], target)

    def other(d):
        return (z + d) % quads * 4 + y * 2 + x

    @pl.when(step == 0)
    def _():
        for c in range(chunks):
            load_weight(c).start()
        for i in range(panel):
            local_token(i).start()
        barrier = pltpu.get_barrier_semaphore()
        peers = [(x_row, col), (y_row, col), (row, 1 - col)]
        peers += [(other(d), col) for d in range(1, quads)]
        for peer in peers:
            pl.semaphore_signal(barrier, inc=1, device_id=peer, device_id_type=MESH)
        pl.semaphore_wait(barrier, len(peers))
        for i in range(panel):
            far_token(i).start()

    def bias_moves(i):
        if i == 0:
            swap(b_ref, bx, 0, x_row).start()
        elif i == 1:
            swap(b_ref, bx, 0, x_row).wait()
            by_out[...] = b_ref[...] + bx[...]
            swap(by_out, by, 1, y_row).start()
        elif i == 2:
            swap(by_out, by, 1, y_row).wait()
            bz_out[...] = by_out[...] + by[...]
            for d in range(1, quads):
                swap(bz_out, bz.at[d - 1], d + 1, other(d)).start()
        else:
            total = bz_out[...]
            for d in range(1, quads):
                swap(bz_out, bz.at[d - 1], d + 1, other(d)).wait()
                total += bz[d - 1]
            bout_ref[...] = total

    for j in range(2):
        now = 2 * step + j

        def on(offset, do, *more):
            if offset % 2 != j:
                return
            m = now - offset

            @pl.when((m >= 0) & (m < span * chunks) & (m % span == 0))
            def _():
                do(m // span, *more)

        for i in reversed(range(quads)):
            on(hop * (i + 1), gather_hop, i)

        def own(c):
            load_weight(c).wait()
            gather_near(c).start()

        on(0, own)
        if begin % 2 == j:
            @pl.when(now == begin)
            def _():
                here = table.at[pl.ds(col * panel, panel)]
                pltpu.make_async_copy(here, here, tl_s).wait()
                come = table.at[pl.ds((1 - col) * panel, panel)]
                pltpu.make_async_copy(come, come, t_r).wait()

        on(begin + span + hop * (quads + 1), scatter_last)
        for i in range(quads):
            on(begin + span + hop * (quads - i), scatter_hop, i)
        on(begin + span, scatter_first)
        for i in range(4):
            if (last + i * hop) % 2 == j:
                pl.when(now == last + i * hop)(functools.partial(bias_moves, i))
        on(begin, gathered)

        @pl.when((now >= begin) & (now < last))
        def _():
            compute(now - begin, j)

    @pl.when(step == pl.num_programs(0) - 1)
    def _():
        mine = table.at[pl.ds(col * panel, panel)]
        pltpu.make_async_copy(mine, mine, t_s).wait()
        link(brecv, brecv, gb_s, gb_r.at[0], x_row).wait_send()
        link(arecv, arecv, ga_s, ga_r.at[0, 0], x_row).wait_send()
        link(psend, psend, ra_s, ra_r.at[0, 0], x_row).wait_send()
        link(bsend, bsend, rb_s, rb_r.at[0], x_row).wait_send()

        @pl.loop(0, chunks)
        def _(c):
            for plane in range(quads):
                pl.when((z < quads - 1) & (plane <= z))(
                    lambda plane=plane: gather_z(c, plane, 1).wait_send())
                pl.when((z > 0) & (plane >= z))(
                    lambda plane=plane: gather_z(c, plane, 0).wait_send())
                pl.when(plane != z)(
                    lambda plane=plane: scatter_z(c, plane, 1, plane).wait_send())


def first_block(quads, hop):
    return (hop * (quads + 1) + 1) // 2 * 2


def fused(pat, tokens, weights, bias, grad_act, quads, scale):
    tok, hidden = grad_act.shape
    blocks = hidden // BLK
    pairs = blocks // 2
    total_rows = weights.shape[0]
    blk_rows = total_rows // blocks
    chunks = next(c for c in (12, 8, 6, 4, 3, 2, 1) if pairs % c == 0)
    n = total_rows // chunks
    hop = 3
    rows = quads * 4
    begin = first_block(quads, hop)
    span = blocks // chunks
    steps = (begin + blocks + hop * (quads + 1)) // 2 + 1
    at = lambda i: jnp.minimum(jnp.maximum(i - begin // 2, 0), pairs - 1)
    wide = lambda m: pl.BlockSpec((m, 2 * BLK), lambda i, p: (0, at(i)))
    fixed = lambda *s: pl.BlockSpec(s, lambda i, p: (0, 0))
    any_spec = pl.BlockSpec(memory_space=pl.ANY)
    dma = pltpu.SemaphoreType.DMA
    bf = lambda *s: pltpu.VMEM(s, jnp.bfloat16)
    f32 = lambda *s: pltpu.VMEM(s, jnp.float32)
    b = (blocks, BLK)
    return pl.pallas_call(
        functools.partial(fused_kernel, quads, chunks, blk_rows, scale, hop),
        out_shape=(
            jax.ShapeDtypeStruct((tok, hidden), jnp.bfloat16),
            jax.ShapeDtypeStruct((total_rows, BLK), jnp.float32),
            jax.ShapeDtypeStruct(b, jnp.float32),
        ),
        grid_spec=pltpu.PrefetchScalarGridSpec(
            num_scalar_prefetch=1, grid=(steps,),
            in_specs=[any_spec, any_spec, wide(1), wide(tok)],
            out_specs=[wide(tok), fixed(total_rows, BLK), fixed(*b)],
            scratch_shapes=[
                bf(2 * tokens.shape[1] // BLK, tok, BLK), bf(chunks, rows, n, BLK),
                f32(chunks, rows, n, BLK), bf(chunks, 2 * quads, n, BLK),
                bf(chunks, 2 * quads, n, BLK), bf(chunks, 2 * quads, n, BLK),
                bf(chunks, 2 * quads + 2, n, BLK), bf(chunks, n, BLK), bf(chunks, n, BLK),
                f32(*b), f32(*b), f32(*b), f32(*b), f32(quads - 1, *b), f32(*b),
                dma, dma, dma, dma((chunks,)), dma, dma((chunks,)),
                dma((chunks, 2, quads)), dma((chunks, quads)), dma, dma((chunks, quads)),
                dma, dma((chunks, quads)), dma((chunks, quads)), dma((chunks, quads + 1)),
                dma, dma((chunks,)), dma((quads + 1,)), dma((quads + 1,)),
            ],
        ),
        compiler_params=pltpu.CompilerParams(collective_id=0, has_side_effects=True,
                                             vmem_limit_bytes=VMEM_LIMIT),
    )(pat, tokens, weights.reshape(chunks, n, BLK), bias, grad_act)


def kernel_body(tokens, w_blocks, hidden_bias, pattern, grad_act):
    tok_rows = tokens.shape[0]
    local_blocks, width = w_blocks.shape
    rows = lax.axis_size("row")
    scale = 1.0 / math.sqrt(tok_rows * rows)
    flat = w_blocks.reshape(local_blocks * width // BLK, BLK)
    activation, weight_grad, bias_grad = fused(
        pattern.reshape(-1), tokens, flat, hidden_bias.reshape(1, -1), grad_act, rows // 4, scale)
    return activation, weight_grad.reshape(local_blocks, width), bias_grad.reshape(-1)


def body(tokens, w_blocks, hidden_bias, pattern, grad_act):
    rows = lax.axis_size("row")
    piece = w_blocks.shape[1] // BLK
    fits = lax.axis_size("col") == 2 and rows % 4 == 0 and rows > 4
    fits = fits and piece % 8 == 0 and w_blocks.shape[0] % 8 == 0
    run = kernel_body if fits else plain_body
    return run(tokens, w_blocks, hidden_bias, pattern, grad_act)


def solution(mesh):
    return jax.shard_map(
        body,
        mesh=mesh,
        in_specs=(P("row", "col"), P("col", "row"), P("col"), P(), P("row", "col")),
        out_specs=(P("row", "col"), P("col", "row"), P("col")),
        check_vma=False,
    )
```

time: 188 us -> 150 us (0.80)
  Pallas kernels: 173 us -> 135 us
    pallas_call x1 -> x0, Pallas kernels: 73.5 us -> none  [gather(): pl.pallas_call(functools.partial(gather_kernel, quads), out_shape=(jax.Sh...]
    pallas_call x1, Pallas kernels: 99.2 us -> 135 us  [fused(): pl.pallas_call(functools.partial(fused_kernel, quads, chunks, blk_rows, s...]
    another operation x0 -> x1, local copies, waits for them, and re-layouts: none -> 2.03 us  [fused(): weights.reshape(chunks, n, BLK)]
    reshape x2 -> x1, local copies, waits for them, and re-layouts: 2.72 us -> 0.75 us  [kernel_body(): pattern.reshape(-1)]
    unnamed x6 -> x5, local copies, waits for them, and re-layouts: 7.53 us -> 7.64 us
where the time goes in v1:
time: 150 us
  Pallas kernels  135 us (90%)
  local copies, waits for them, and re-layouts  14 us (9%)
    pallas_call x1, Pallas kernels, fused(): pl.pallas_call(functools.partial(fused_kernel, quads, chunks, blk_rows, s...  135 us
    unnamed x5, local copies, waits for them, and re-layouts  7.64 us

profile of v1, /device:TPU:0, one launch (start us, length us, event | category | flops | bytes accessed | tf_op | source)
XLA Modules:
  0.0 150.0 jit_solution(8011095589884471291)
XLA Ops:
  0.6 1.3 reshape.19.bias_ref
  2.0 0.8 copy.8
  2.7 0.8 reshape.18.pat_ref
  3.5 2.0 %reshape_reshape.3.w_ref = bf16[12,160,128]{2,1,0:T(8,128)(2,1)} reshape(bf16[48,5120]{1,0:T(8,128)(2,1)} %param.6) | data formatting | bytes 983040 | tf_op jit(solution)/shard_map/reshape;reshape | solution.py:421
  5.5 135.3 %shard_map.76 = (bf16[512,6144]{1,0:T(8,128)(2,1)}, f32[1920,128]{1,0:T(8,128)}, f32[48,128]{1,0:T(8,128)}) custom-call(s32[480]{0:T(512)} %reshape.18.pat_ref, bf16[512,3072]{1,0:T(8,128)(2,1)} %tok_ref.1, bf16[12,160,128]{2,1,0:T(8,128)(2,1)} %reshape_reshape.3.w_ref, bf16[1,6144]{1,0:T(2,128)(2,1)} %reshape.19.bias_ref, bf16[512,6144]{1,0:T(8,128)(2,1)} %grad_ref.1), custom_call_target="tpu_custom_call" | custom-call | tf_op jit(solution)/shard_map/pallas_call | solution.py:396
  140.8 2.3 %reshape.20 = f32[48,5120]{1,0:T(8,128)} reshape(f32[1920,128]{1,0:T(8,128)} %get-tuple-element.7) | data formatting | bytes 1966080 | tf_op jit(solution)/shard_map/reshape | solution.py:432
  143.1 0.0 copy-start
  143.1 6.2 %copy.11 = bf16[512,6144]{1,0:T(8,128)(2,1)} copy(bf16[512,6144]{1,0:T(8,128)(2,1)} %get-tuple-element.12) | data formatting | bytes 12582912
  149.3 0.0 copy-done
  149.3 0.6 copy.12
Async XLA Ops:
  143.1 6.2 %copy-start = (f32[48,128]{1,0:T(8,128)S(1)}, f32[48,128]{1,0:T(8,128)}, u32[]{:S(2)}) copy-start(f32[48,128]{1,0:T(8,128)} %get-tuple-element.8) | copy-start | bytes 73732

commit v2 on v1

--- a/solution.py
+++ b/solution.py
@@ -13,7 +13,7 @@
 GLOB = 2
 KSLOT = 5
 MESH = pl.DeviceIdType.MESH
-VMEM_LIMIT = 60 * 1024 * 1024
+VMEM_LIMIT = 50 * 1024 * 1024
 
 
 def from_behind(block, axis, distance):
@@ -70,12 +70,12 @@
     return (activation, weight_grad, bias_grad)
 
 
-def fused_kernel(quads, chunks, blk_rows, scale, hop,
+def fused_kernel(quads, chunks, blk_rows, scale, plan,
                  pat_ref, tok_ref, w_ref, bias_ref, grad_ref,
                  act_ref, out_ref, bout_ref,
                  table, wbuf, part, psend, arecv, zout, zrecv, bsend, brecv,
-                 b_ref, bx, by, by_out, bz, bz_out,
-                 tl_s, t_s, t_r, lw_s, gb_s, gb_r, gz_s, gz_r, ga_s, ga_r,
+                 lines, shift, b_ref, bx, by, by_out, bz, bz_out,
+                 tl_s, t_s, t_r, gb_s, gb_r, gz_s, gz_r, ga_s, ga_r,
                  ra_s, ra_r, rz_s, rz_r, rb_s, rb_r, b_s, b_r):
     step = pl.program_id(0)
     n = wbuf.shape[2]
@@ -88,8 +88,9 @@
     x_row = z * 4 + y * 2 + 1 - x
     y_row = z * 4 + (1 - y) * 2 + x
     panel = tok_ref.shape[1] // BLK
-    begin = first_block(quads, hop)
+    gather_at, begin, scatter_at = plan
     last = begin + 2 * pairs
+    after = begin + span
 
     def link(src, dst, s, r, target):
         return pltpu.make_async_remote_copy(
@@ -117,10 +118,6 @@
 
     def spot(side, plane, b):
         return (side * quads + plane) * 2 + b
-
-    def load_weight(c):
-        a, b, _, _ = sides(c)
-        return pltpu.make_async_copy(w_ref.at[c], wbuf.at[c, spot(a, z, b)], lw_s.at[c])
 
     def gather_near(c):
         a, b, _, b_row = sides(c)
@@ -235,7 +232,7 @@
 
     def compute(block, j):
         c = block // span
-        base = (col * 2 * pairs + block) * KSLOT
+        base = col * 2 * pairs + block
         skip = j * blk_rows // 16 * 16
         tall = -(-(j * blk_rows - skip + blk_rows) // 16) * 16
         cut = slice(j * blk_rows - skip, j * blk_rows - skip + blk_rows)
@@ -249,10 +246,10 @@
         w = [wbuf[c, s, pl.ds(at, tall), :].astype(jnp.float32)[cut] for s in spots]
         w = jnp.concatenate(w, axis=0).astype(jnp.bfloat16)
         piece = pl.ds(j * BLK, BLK)
-        picks = [table[pat_ref[base + s]] for s in range(KSLOT)]
+        picks = [table[pat_ref[s, base]] for s in range(KSLOT)]
         sel = jnp.concatenate(picks, axis=1)
         v = jnp.dot(sel, w, preferred_element_type=jnp.float32)
-        v = v + bias_ref[:, piece].astype(jnp.float32)
+        v = v + shift[pl.ds(block, 1), :]
         e = math.sqrt(2.0 / math.pi)
         sq = v * v
         t = jnp.tanh(v * (e + (e * 0.044715) * sq))
@@ -275,10 +272,16 @@
 
     @pl.when(step == 0)
     def _():
-        for c in range(chunks):
-            load_weight(c).start()
         for i in range(panel):
             local_token(i).start()
+        wide = w_ref.shape[1] // BLK
+        for i in range(wide):
+            lines[pl.ds(i, 2 * pairs, stride=wide), :] = (
+                w_ref[:, i * BLK:(i + 1) * BLK].astype(jnp.float32))
+        for c in range(chunks):
+            a, b, _, _ = sides(c)
+            wbuf[c, spot(a, z, b)] = lines[c * n:(c + 1) * n, :].astype(jnp.bfloat16)
+        shift[...] = bias_ref[...].astype(jnp.float32).reshape(2 * pairs, BLK)
         barrier = pltpu.get_barrier_semaphore()
         peers = [(x_row, col), (y_row, col), (row, 1 - col)]
         peers += [(other(d), col) for d in range(1, quads)]
@@ -307,6 +310,14 @@
                 total += bz[d - 1]
             bout_ref[...] = total
 
+    def own(c):
+        gather_near(c).start()
+
+    @pl.when(step == 0)
+    def _():
+        for c in range(min(chunks, -(gather_at[0] // span))):
+            own(c)
+
     for j in range(2):
         now = 2 * step + j
 
@@ -320,13 +331,8 @@
                 do(m // span, *more)
 
         for i in reversed(range(quads)):
-            on(hop * (i + 1), gather_hop, i)
-
-        def own(c):
-            load_weight(c).wait()
-            gather_near(c).start()
-
-        on(0, own)
+            on(gather_at[i + 1], gather_hop, i)
+        on(gather_at[0], own)
         if begin % 2 == j:
             @pl.when(now == begin)
             def _():
@@ -335,13 +341,13 @@
                 come = table.at[pl.ds((1 - col) * panel, panel)]
                 pltpu.make_async_copy(come, come, t_r).wait()
 
-        on(begin + span + hop * (quads + 1), scatter_last)
+        on(after + scatter_at[quads + 1], scatter_last)
         for i in range(quads):
-            on(begin + span + hop * (quads - i), scatter_hop, i)
-        on(begin + span, scatter_first)
+            on(after + scatter_at[quads - i], scatter_hop, i)
+        on(after + scatter_at[0], scatter_first)
         for i in range(4):
-            if (last + i * hop) % 2 == j:
-                pl.when(now == last + i * hop)(functools.partial(bias_moves, i))
+            if (last + 3 * i) % 2 == j:
+                pl.when(now == last + 3 * i)(functools.partial(bias_moves, i))
         on(begin, gathered)
 
         @pl.when((now >= begin) & (now < last))
@@ -368,49 +374,53 @@
                     lambda plane=plane: scatter_z(c, plane, 1, plane).wait_send())
 
 
-def first_block(quads, hop):
-    return (hop * (quads + 1) + 1) // 2 * 2
+def plan_of(quads):
+    if quads == 4:
+        return (-27, 5, 12, 15, 18), 20, (0, 3, 4, 8, 15, 21)
+    gather_at = tuple(3 * i for i in range(quads + 1))
+    return gather_at, 4 * quads, tuple(3 * i for i in range(quads + 2))
 
 
 def fused(pat, tokens, weights, bias, grad_act, quads, scale):
     tok, hidden = grad_act.shape
     blocks = hidden // BLK
     pairs = blocks // 2
-    total_rows = weights.shape[0]
+    total_rows = weights.size // BLK
     blk_rows = total_rows // blocks
-    chunks = next(c for c in (12, 8, 6, 4, 3, 2, 1) if pairs % c == 0)
+    chunks = next(c for c in (24, 12, 8, 6, 4, 3, 2, 1) if pairs % c == 0)
     n = total_rows // chunks
-    hop = 3
+    plan = plan_of(quads)
     rows = quads * 4
-    begin = first_block(quads, hop)
+    begin = plan[1]
     span = blocks // chunks
-    steps = (begin + blocks + hop * (quads + 1)) // 2 + 1
+    steps = (begin + blocks + max(plan[2][-1], 9)) // 2 + 1
     at = lambda i: jnp.minimum(jnp.maximum(i - begin // 2, 0), pairs - 1)
     wide = lambda m: pl.BlockSpec((m, 2 * BLK), lambda i, p: (0, at(i)))
     fixed = lambda *s: pl.BlockSpec(s, lambda i, p: (0, 0))
     any_spec = pl.BlockSpec(memory_space=pl.ANY)
+    vmem = pl.BlockSpec(memory_space=pltpu.VMEM)
     dma = pltpu.SemaphoreType.DMA
     bf = lambda *s: pltpu.VMEM(s, jnp.bfloat16)
     f32 = lambda *s: pltpu.VMEM(s, jnp.float32)
     b = (blocks, BLK)
     return pl.pallas_call(
-        functools.partial(fused_kernel, quads, chunks, blk_rows, scale, hop),
+        functools.partial(fused_kernel, quads, chunks, blk_rows, scale, plan),
         out_shape=(
-            jax.ShapeDtypeStruct((tok, hidden), jnp.bfloat16),
-            jax.ShapeDtypeStruct((total_rows, BLK), jnp.float32),
-            jax.ShapeDtypeStruct(b, jnp.float32),
+            pltpu.VMEM((tok, hidden), jnp.bfloat16),
+            pltpu.VMEM((total_rows, BLK), jnp.float32),
+            pltpu.VMEM(b, jnp.float32),
         ),
         grid_spec=pltpu.PrefetchScalarGridSpec(
             num_scalar_prefetch=1, grid=(steps,),
-            in_specs=[any_spec, any_spec, wide(1), wide(tok)],
+            in_specs=[any_spec, vmem, vmem, wide(tok)],
             out_specs=[wide(tok), fixed(total_rows, BLK), fixed(*b)],
             scratch_shapes=[
                 bf(2 * tokens.shape[1] // BLK, tok, BLK), bf(chunks, rows, n, BLK),
                 f32(chunks, rows, n, BLK), bf(chunks, 2 * quads, n, BLK),
                 bf(chunks, 2 * quads, n, BLK), bf(chunks, 2 * quads, n, BLK),
                 bf(chunks, 2 * quads + 2, n, BLK), bf(chunks, n, BLK), bf(chunks, n, BLK),
-                f32(*b), f32(*b), f32(*b), f32(*b), f32(quads - 1, *b), f32(*b),
-                dma, dma, dma, dma((chunks,)), dma, dma((chunks,)),
+                f32(total_rows, BLK), f32(*b), f32(*b), f32(*b), f32(*b), f32(*b), f32(quads - 1, *b), f32(*b),
+                dma, dma, dma, dma, dma((chunks,)),
                 dma((chunks, 2, quads)), dma((chunks, quads)), dma, dma((chunks, quads)),
                 dma, dma((chunks, quads)), dma((chunks, quads)), dma((chunks, quads + 1)),
                 dma, dma((chunks,)), dma((quads + 1,)), dma((quads + 1,)),
@@ -418,18 +428,52 @@
         ),
         compiler_params=pltpu.CompilerParams(collective_id=0, has_side_effects=True,
                                              vmem_limit_bytes=VMEM_LIMIT),
-    )(pat, tokens, weights.reshape(chunks, n, BLK), bias, grad_act)
+    )(pat, tokens, weights, bias, grad_act)
+
+
+def finish_kernel(parts, act_in, grad_in, bias_in, act_out, grad_out, bias_out, sems):
+    tall = act_in.shape[0] // parts
+    copies = [pltpu.make_async_copy(bias_in, bias_out, sems.at[parts])]
+    copies[0].start()
+    for i in range(parts):
+        cut = pl.ds(i * tall, tall)
+        copies.append(pltpu.make_async_copy(act_in.at[cut], act_out.at[cut], sems.at[i]))
+        copies[-1].start()
+    blocks, width = grad_out.shape
+    each = width // BLK
+    for i in range(each):
+        grad_out[:, i * BLK:(i + 1) * BLK] = grad_in[pl.ds(i, blocks, stride=each), :]
+    for copy in copies:
+        copy.wait()
+
+
+def finish(act, grad, bias, blocks):
+    parts = 4
+    any_spec = pl.BlockSpec(memory_space=pl.ANY)
+    vmem = pl.BlockSpec(memory_space=pltpu.VMEM)
+    return pl.pallas_call(
+        functools.partial(finish_kernel, parts),
+        out_shape=(
+            jax.ShapeDtypeStruct(act.shape, act.dtype),
+            jax.ShapeDtypeStruct((blocks, grad.size // blocks), grad.dtype),
+            jax.ShapeDtypeStruct(bias.shape, bias.dtype),
+        ),
+        in_specs=[any_spec, vmem, any_spec],
+        out_specs=(any_spec, vmem, any_spec),
+        scratch_shapes=[pltpu.SemaphoreType.DMA((parts + 1,))],
+        compiler_params=pltpu.CompilerParams(vmem_limit_bytes=8 * 1024 * 1024),
+    )(act, grad, bias)
 
 
 def kernel_body(tokens, w_blocks, hidden_bias, pattern, grad_act):
     tok_rows = tokens.shape[0]
-    local_blocks, width = w_blocks.shape
+    local_blocks = w_blocks.shape[0]
     rows = lax.axis_size("row")
     scale = 1.0 / math.sqrt(tok_rows * rows)
-    flat = w_blocks.reshape(local_blocks * width // BLK, BLK)
     activation, weight_grad, bias_grad = fused(
-        pattern.reshape(-1), tokens, flat, hidden_bias.reshape(1, -1), grad_act, rows // 4, scale)
-    return activation, weight_grad.reshape(local_blocks, width), bias_grad.reshape(-1)
+        pattern.T, tokens, w_blocks, hidden_bias, grad_act, rows // 4, scale)
+    activation, weight_grad, bias_grad = finish(activation, weight_grad, bias_grad, local_blocks)
+    return activation, weight_grad, bias_grad.reshape(-1)
 
 
 def body(tokens, w_blocks, hidden_bias, pattern, grad_act):

time: 150 us -> 133 us (0.89)
  local copies, waits for them, and re-layouts: 14 us -> 0 us
  Pallas kernels: 135 us -> 133 us
    unnamed x5 -> x0, local copies, waits for them, and re-layouts: 7.64 us -> none
    pallas_call x1, Pallas kernels: 135 us -> 129 us  [fused(): pl.pallas_call(functools.partial(fused_kernel, quads, chunks, blk_rows, s...]
    reshape x3 -> x0, local copies, waits for them, and re-layouts: 4.38 us -> none  [the longest x1 2.3 us: kernel_body(): weight_grad.reshape(local_blocks, width)]
    pallas_call x0 -> x1, Pallas kernels: none -> 3.69 us  [finish(): pl.pallas_call(functools.partial(finish_kernel, parts), out_shape=(jax.Sh...]
    another operation x1 -> x0, local copies, waits for them, and re-layouts: 2.03 us -> none  [fused(): weights.reshape(chunks, n, BLK)]
where the time goes in v2:
time: 133 us
  Pallas kernels  133 us (100%)
    pallas_call x1, Pallas kernels, fused(): pl.pallas_call(functools.partial(fused_kernel, quads, chunks, blk_rows, s...  129 us
    pallas_call x1, Pallas kernels, finish(): pl.pallas_call(functools.partial(finish_kernel, parts), out_shape=(jax.Sh...  3.69 us

profile of v2, /device:TPU:0, one launch (start us, length us, event | category | flops | bytes accessed | tf_op | source)
XLA Modules:
  0.0 133.3 jit_solution(15999280982326299526)
XLA Ops:
  0.6 128.9 %shard_map.76 = (bf16[512,6144]{1,0:T(8,128)(2,1)S(1)}, f32[1920,128]{1,0:T(8,128)S(1)}, f32[48,128]{1,0:T(8,128)S(1)}) custom-call(s32[5,96]{1,0:T(8,128)} %bitcast.2, bf16[512,3072]{1,0:T(8,128)(2,1)} %tok_ref.1, bf16[48,5120]{1,0:T(8,128)(2,1)} %w_ref.1, bf16[6144]{0:T(1024)(128)(2,1)} %bias_ref.1, bf16[512,6144]{1,0:T(8,128)(2,1)} %grad_ref.1), custom_call_target="tpu_custom_call" | custom-call | tf_op jit(solution)/shard_map/pallas_call | solution.py:406
  129.6 3.7 %shard_map.77 = (bf16[512,6144]{1,0:T(8,128)(2,1)}, f32[48,5120]{1,0:T(8,128)}, f32[48,128]{1,0:T(8,128)}) custom-call(bf16[512,6144]{1,0:T(8,128)(2,1)S(1)} %get-tuple-element.9.act_in, f32[1920,128]{1,0:T(8,128)S(1)} %get-tuple-element.10.grad_in, f32[48,128]{1,0:T(8,128)S(1)} %get-tuple-element.11.bias_in), custom_call_target="tpu_custom_call" | custom-call | tf_op jit(solution)/shard_map/pallas_call | solution.py:454
